TPU v7x, 256 devices: a whole 4x4x8 slice. The times are simulated.
256 devices in a mesh: row: 16 (over x, z_lo, core), col: 16 (over z_hi, y).
Axes of the slice: x: 4, y: 4, z: 8 (z_hi: 4, z_lo: 2; z = z_hi * 2 + z_lo), core: 2. Of those that a mesh axis runs over, the one named last changes fastest.
Arguments:
- iterate: bfloat16 [4096, 8192], P('row', 'col'), may hold values from -0.5 to 0.5, as said below
Outputs:
- update: float32 [4096, 8192], P('row', 'col')
Inputs may be any that keep to these rules, and one draw needn't show every extreme that they name: One iterate of the orthogonalization.
All inputs are finite; a program needn't handle non-finite values.
Results may differ from a plain program's by a relative error of at most 0.0041.
Values may be sent and summed in bfloat16 or wider, within the bound.
No kernel may reach another device: no remote copies, remote signals or barrier semaphores. Data moves between devices by JAX's collectives and lax.ppermute only.
A program may use at most 64 MiB of HBM per device.

v0:
```python
import math
import jax
import jax.numpy as jnp
from jax import lax
from jax.sharding import Mesh
from jax.sharding import PartitionSpec as P

COLS = 8192
coef_a = 3.4445
coef_b = -4.775
coef_c = 2.0315
ROW = ("x", "zl", "core")
COL = ("zh", "y")
BF, F32 = (jnp.bfloat16, jnp.float32)


def swap(array, axis):
    return lax.ppermute(array, axis, [(0, 1), (1, 0)])


def send(array, axis, k):
    return lax.ppermute(array, axis, [(i, (i + k) % 4) for i in range(4)]) if k else array


def fetch(array, axis, k):
    return send(array, axis, (4 - k) % 4)


def add(got):
    got = [g.astype(F32) for g in got]
    return (got[0] + got[1] + (got[2] + got[3])).astype(BF)


def trade(array, axis, k):
    return lax.ppermute(array, axis, [(i, i ^ k) for i in range(4)])


def scatter_pairs(pieces, axis):
    return [pieces[0]] + [trade(pieces[k], axis, k) for k in (1, 3, 2)]


def chunks(array):
    return jnp.split(array, 4, axis=0)


def window(parts, first, count):
    rows = parts[0].shape[0]
    ring = jnp.concatenate([*parts, *parts[: count - 1]], axis=0)
    return lax.dynamic_slice_in_dim(ring, first * rows, count * rows, 0)


def matmul(a, b, dims):
    return lax.dot_general(a, b, (dims, ((), ())), preferred_element_type=F32)


def pair_of(block):
    far = fetch(block, "x", 2)
    return (jnp.concatenate([block, swap(block, "zl")], axis=0), far)


def late_blocks(pair, far):
    return [trade(pair, "x", 1), trade(pair, "x", 3), swap(far, "zl")]


def core_sum(products):
    mine = jnp.concatenate([m for m, _ in products], axis=0)
    other = jnp.concatenate([o for _, o in products], axis=0)
    return mine + swap(other, "core")


def per_device(iterate):
    y, zh = (lax.axis_index("y"), lax.axis_index("zh"))
    back = lax.rem(4 - y, 4)
    other = swap(iterate, "core")
    pair, far = pair_of(iterate)
    own = [jnp.concatenate(rows, axis=0) for rows in zip(chunks(iterate), chunks(other))]
    own = jnp.stack(own).reshape(4, 4, 32, 512)
    own = [lax.dynamic_slice_in_dim(own, zh ^ k, 1, 1) for k in range(4)]
    own = jnp.concatenate(own, axis=1).reshape(512, 512)
    turned = [lax.dynamic_slice_in_dim(own, (y ^ k) * 128, 128) for k in range(4)]
    turned = jnp.concatenate(turned, axis=0)
    pair, own, turned = lax.optimization_barrier((pair, own, turned))
    early = lax.optimization_barrier(jnp.concatenate([pair, far], axis=0))
    pieces = matmul(own, early, ((1,), (1,))).astype(BF)
    late = late_blocks(pair, far)
    first = add(lax.all_to_all(pieces.reshape(4, 128, 768), "y", 0, 0))
    panel = lax.optimization_barrier(jnp.concatenate(late, axis=0))
    pieces = [matmul(rows, panel, ((1,), (1,))).astype(BF) for rows in chunks(turned)]
    pieces[0] = lax.optimization_barrier(pieces[0])
    second = add(scatter_pairs(pieces, "y"))
    part = jnp.concatenate([first, second], axis=1)
    panel = jnp.concatenate([early, panel], axis=0)
    part = add(scatter_pairs(chunks(part), "zh"))
    near = lax.all_gather(part, "zh", axis=0, tiled=True)
    after, before = (fetch(near, "y", 1), fetch(near, "y", 3))
    sent = lax.optimization_barrier((after[:64], before[64:]))
    far = lax.optimization_barrier((fetch(sent[0], "y", 1), fetch(sent[1], "y", 3)))

    def product(rows):
        return matmul(rows, panel, ((1,), (0,)))

    first = core_sum([(m[:64], m[64:]) for m in map(product, (near, after, before))])
    second = core_sum([(product(far[0]), product(far[1]))])
    inner = window([first[:64], first[64:128], second, first[128:]], back, 4)
    pair, last = pair_of(inner.astype(BF))
    pair, *late = lax.optimization_barrier([pair, last, *late_blocks(pair, last)])
    panels = (jnp.concatenate([pair, late[0]], axis=0), jnp.concatenate(late[1:], axis=0))
    gram = [(near[:64], near[64:]), (after[:64], after[64:]), far, (before[:64], before[64:])]
    mixed = []
    for rows in zip(*gram):
        rows = window(rows, back, 4)
        halves = (rows[:, :768], rows[:, 768:])
        mixed.append(sum((matmul(h, panel, ((1,), (0,))) for h, panel in zip(halves, panels))))
    mixed = mixed[0] + swap(mixed[1], "core")
    mine = iterate.astype(F32)
    return math.sqrt(COLS) * (coef_a * mine + (coef_b * inner + coef_c * mixed))


def solution(mesh):
    fine = Mesh(mesh.devices.reshape(4, 2, 2, 4, 4), (*ROW, *COL))
    placed = P(ROW, COL)
    return jax.shard_map(
        per_device, mesh=fine, in_specs=(placed,), out_specs=placed, check_vma=False
    )
```

profile of v0, /device:TPU:1, one launch (start us, length us, event | category | flops | bytes accessed | tf_op | source)
XLA Modules:
  0.0 139.4 jit_solution(9716099758347293773)
XLA Ops:
  0.0 3.2 %collective-permute-start.1 = (bf16[256,512]{1,0:T(8,128)(2,1)}, bf16[256,512]{1,0:T(8,128)(2,1)S(1)}, u32[]{:S(2)}, u32[]{:S(2)}) collective-permute-start(bf16[256,512]{1,0:T(8,128)(2,1)} %param.1), channel_id=1, source_target_pairs={{0,16},{16,0},{1,17},{17,1},{2,18},{18,2},{3,19},{19,3},{4,20},{20... | collective-permute-start | bytes 786440 | tf_op jit(solution)/shard_map/ppermute | solution.py:18
  3.2 2.6 %collective-permute-start.2 = (bf16[256,512]{1,0:T(8,128)(2,1)}, bf16[256,512]{1,0:T(8,128)(2,1)}, u32[]{:S(2)}, u32[]{:S(2)}) collective-permute-start(bf16[256,512]{1,0:T(8,128)(2,1)} %param.1), channel_id=1, source_target_pairs={{0,128},{64,192},{128,0},{192,64},{1,129},{65,193},{129,1},{193,65... | collective-permute-start | bytes 786440 | tf_op jit(solution)/shard_map/ppermute | solution.py:22
  7.3 4.2 %collective-permute-done = bf16[256,512]{1,0:T(8,128)(2,1)S(1)} collective-permute-done((bf16[256,512]{1,0:T(8,128)(2,1)}, bf16[256,512]{1,0:T(8,128)(2,1)S(1)}, u32[]{:S(2)}, u32[]{:S(2)}) %collective-permute-start) | collective-permute-done | bytes 262176 | tf_op jit(solution)/shard_map/ppermute | solution.py:18
  17.2 4.2 %all-to-all-start = ((bf16[4,128,768]{2,1,0:T(8,128)(2,1)}), bf16[4,128,768]{2,1,0:T(8,128)(2,1)S(1)}, u32[]{:S(2)}, u32[]{:S(2)}) async-start(bf16[4,128,768]{2,1,0:T(8,128)(2,1)} %bitcast.25), calls=%async_computation | async-start | bytes 1572864 | tf_op jit(solution)/shard_map/all_to_all | solution.py:86
  21.3 3.2 %collective-permute-done.3 = bf16[512,512]{1,0:T(8,128)(2,1)S(1)} collective-permute-done((bf16[512,512]{1,0:T(8,128)(2,1)S(1)}, bf16[512,512]{1,0:T(8,128)(2,1)S(1)}, u32[]{:S(2)}, u32[]{:S(2)}) %collective-permute-start.3) | collective-permute-done | bytes 524320 | tf_op jit(solution)/shard_map/ppermute | solution.py:35
  29.7 1.9 %collective-permute-start.7 = (bf16[128,1280]{1,0:T(8,128)(2,1)S(1)}, bf16[128,1280]{1,0:T(8,128)(2,1)}, u32[]{:S(2)}, u32[]{:S(2)}) collective-permute-start(bf16[128,1280]{1,0:T(8,128)(2,1)S(1)} %convolution_convert_fusion.1), channel_id=1, source_target_pairs={{0,3},{1,2},{2,1},{3,0},{4,7},{5,6},{6,5},{7,4},{8,11},{9,10},{10,... | collective-permute-start | bytes 983048 | tf_op jit(solution)/shard_map/ppermute | solution.py:35
  34.3 4.2 %collective-permute-done.6 = bf16[128,1280]{1,0:T(8,128)(2,1)} collective-permute-done((bf16[128,1280]{1,0:T(8,128)(2,1)}, bf16[128,1280]{1,0:T(8,128)(2,1)}, u32[]{:S(2)}, u32[]{:S(2)}) %collective-permute-start.6) | collective-permute-done | bytes 327712 | tf_op jit(solution)/shard_map/ppermute | solution.py:35
  39.3 7.1 %collective-permute-done.8 = bf16[128,1280]{1,0:T(8,128)(2,1)} collective-permute-done((bf16[128,1280]{1,0:T(8,128)(2,1)}, bf16[128,1280]{1,0:T(8,128)(2,1)}, u32[]{:S(2)}, u32[]{:S(2)}) %collective-permute-start.8) | collective-permute-done | bytes 327712 | tf_op jit(solution)/shard_map/ppermute | solution.py:35
  47.8 4.8 %collective-permute-start.10 = (bf16[32,2048]{1,0:T(8,128)(2,1)S(1)}, bf16[32,2048]{1,0:T(8,128)(2,1)S(1)}, u32[]{:S(2)}, u32[]{:S(2)}) collective-permute-start(bf16[32,2048]{1,0:T(8,128)(2,1)S(1)} %get-tuple-element.37), channel_id=1, source_target_pairs={{0,12},{4,8},{8,4},{12,0},{1,13},{5,9},{9,5},{13,1},{2,14},{6,10},... | collective-permute-start | bytes 393224 | tf_op jit(solution)/shard_map/ppermute | solution.py:35
  52.6 1.6 %collective-permute-start.11 = (bf16[32,2048]{1,0:T(8,128)(2,1)S(1)}, bf16[32,2048]{1,0:T(8,128)(2,1)S(1)}, u32[]{:S(2)}, u32[]{:S(2)}) collective-permute-start(bf16[32,2048]{1,0:T(8,128)(2,1)S(1)} %get-tuple-element.36), channel_id=1, source_target_pairs={{0,8},{4,12},{8,0},{12,4},{1,9},{5,13},{9,1},{13,5},{2,10},{6,14},... | collective-permute-start | bytes 393224 | tf_op jit(solution)/shard_map/ppermute | solution.py:35
  54.8 7.4 %collective-permute-done.10 = bf16[32,2048]{1,0:T(8,128)(2,1)S(1)} collective-permute-done((bf16[32,2048]{1,0:T(8,128)(2,1)S(1)}, bf16[32,2048]{1,0:T(8,128)(2,1)S(1)}, u32[]{:S(2)}, u32[]{:S(2)}) %collective-permute-start.10) | collective-permute-done | bytes 131104 | tf_op jit(solution)/shard_map/ppermute | solution.py:35
  64.2 15.8 %all_gather.3 = bf16[128,2048]{1,0:T(8,128)(2,1)S(1)} all-gather(bf16[32,2048]{1,0:T(8,128)(2,1)S(1)} %add_convert_fusion.2), channel_id=1, replica_groups=mesh['x'=4,'zl'=2,'core'=2,'zh'=4,'y'=4] {'zh'}, dimensions={0}, use_global_device_ids=true | all-gather | bytes 655360 | tf_op jit(solution)/shard_map/all_gather | solution.py:94
  81.5 3.4 %collective-permute-start.13 = (bf16[128,2048]{1,0:T(8,128)(2,1)S(1)}, bf16[128,2048]{1,0:T(8,128)(2,1)S(1)}, u32[]{:S(2)}, u32[]{:S(2)}) collective-permute-start(bf16[128,2048]{1,0:T(8,128)(2,1)S(1)} %all_gather.3), channel_id=1, source_target_pairs={{0,1},{1,2},{2,3},{3,0},{4,5},{5,6},{6,7},{7,4},{8,9},{9,10},{10,1... | collective-permute-start | bytes 1572872 | tf_op jit(solution)/shard_map/ppermute | solution.py:22
  85.5 7.4 %collective-permute-done.13 = bf16[128,2048]{1,0:T(8,128)(2,1)S(1)} collective-permute-done((bf16[128,2048]{1,0:T(8,128)(2,1)S(1)}, bf16[128,2048]{1,0:T(8,128)(2,1)S(1)}, u32[]{:S(2)}, u32[]{:S(2)}) %collective-permute-start.13) | collective-permute-done | bytes 524320 | tf_op jit(solution)/shard_map/ppermute | solution.py:22
  94.0 1.9 %collective-permute-start.15 = (bf16[64,2048]{1,0:T(8,128)(2,1)S(1)}, bf16[64,2048]{1,0:T(8,128)(2,1)S(1)}, u32[]{:S(2)}, u32[]{:S(2)}) collective-permute-start(bf16[64,2048]{1,0:T(8,128)(2,1)S(1)} %get-tuple-element.20), channel_id=1, source_target_pairs={{0,3},{1,0},{2,1},{3,2},{4,7},{5,4},{6,5},{7,6},{8,11},{9,8},{10,9... | collective-permute-start | bytes 786440 | tf_op jit(solution)/shard_map/ppermute | solution.py:22
  96.9 5.3 %collective-permute-start.14 = (f32[192,512]{1,0:T(8,128)S(1)}, f32[192,512]{1,0:T(8,128)S(1)}, u32[]{:S(2)}, u32[]{:S(2)}) collective-permute-start(f32[192,512]{1,0:T(8,128)S(1)} %pad_maximum_fusion.8), channel_id=1, source_target_pairs={{0,16},{16,0},{1,17},{17,1},{2,18},{18,2},{3,19},{19,3},{4,20},{20... | collective-permute-start | bytes 1179656 | tf_op jit(solution)/shard_map/ppermute | solution.py:18
  102.9 5.7 %collective-permute-start.17 = (f32[64,512]{1,0:T(8,128)S(1)}, f32[64,512]{1,0:T(8,128)S(1)}, u32[]{:S(2)}, u32[]{:S(2)}) collective-permute-start(f32[64,512]{1,0:T(8,128)S(1)} %fusion.20), channel_id=1, source_target_pairs={{0,16},{16,0},{1,17},{17,1},{2,18},{18,2},{3,19},{19,3},{4,20},{20... | collective-permute-start | bytes 393224 | tf_op jit(solution)/shard_map/ppermute | solution.py:18
  110.6 4.1 %collective-permute-start.19 = (bf16[256,512]{1,0:T(8,128)(2,1)S(1)}, bf16[256,512]{1,0:T(8,128)(2,1)S(1)}, u32[]{:S(2)}, u32[]{:S(2)}) collective-permute-start(bf16[256,512]{1,0:T(8,128)(2,1)S(1)} %dynamic-slice_convert_fusion), channel_id=1, source_target_pairs={{0,128},{64,192},{128,0},{192,64},{1,129},{65,193},{129,1},{193,65... | collective-permute-start | bytes 786440 | tf_op jit(solution)/shard_map/ppermute | solution.py:22
  114.7 3.1 %collective-permute-done.18 = bf16[256,512]{1,0:T(8,128)(2,1)S(1)} collective-permute-done((bf16[256,512]{1,0:T(8,128)(2,1)S(1)}, bf16[256,512]{1,0:T(8,128)(2,1)S(1)}, u32[]{:S(2)}, u32[]{:S(2)}) %collective-permute-start.18) | collective-permute-done | bytes 262176 | tf_op jit(solution)/shard_map/ppermute | solution.py:18
  119.0 3.5 %collective-permute-start.21 = (bf16[512,512]{1,0:T(8,128)(2,1)S(1)}, bf16[512,512]{1,0:T(8,128)(2,1)S(1)}, u32[]{:S(2)}, u32[]{:S(2)}) collective-permute-start(bf16[512,512]{1,0:T(8,128)(2,1)S(1)} %pad_maximum_fusion.7), channel_id=1, source_target_pairs={{0,192},{64,128},{128,64},{192,0},{1,193},{65,129},{129,65},{193,1... | collective-permute-start | bytes 1572872 | tf_op jit(solution)/shard_map/ppermute | solution.py:35
  122.9 5.7 %collective-permute-done.22 = bf16[256,512]{1,0:T(8,128)(2,1)S(1)} collective-permute-done((bf16[256,512]{1,0:T(8,128)(2,1)S(1)}, bf16[256,512]{1,0:T(8,128)(2,1)S(1)}, u32[]{:S(2)}, u32[]{:S(2)}) %collective-permute-start.22) | collective-permute-done | bytes 262176 | tf_op jit(solution)/shard_map/ppermute | solution.py:18
  128.6 2.7 %collective-permute-done.20 = bf16[512,512]{1,0:T(8,128)(2,1)S(1)} collective-permute-done((bf16[512,512]{1,0:T(8,128)(2,1)S(1)}, bf16[512,512]{1,0:T(8,128)(2,1)S(1)}, u32[]{:S(2)}, u32[]{:S(2)}) %collective-permute-start.20) | collective-permute-done | bytes 524320 | tf_op jit(solution)/shard_map/ppermute | solution.py:35
  131.3 2.0 %collective-permute-done.21 = bf16[512,512]{1,0:T(8,128)(2,1)S(1)} collective-permute-done((bf16[512,512]{1,0:T(8,128)(2,1)S(1)}, bf16[512,512]{1,0:T(8,128)(2,1)S(1)}, u32[]{:S(2)}, u32[]{:S(2)}) %collective-permute-start.21) | collective-permute-done | bytes 524320 | tf_op jit(solution)/shard_map/ppermute | solution.py:35
  134.4 2.2 %collective-permute-start.23 = (f32[256,512]{1,0:T(8,128)S(1)}, f32[256,512]{1,0:T(8,128)S(1)}, u32[]{:S(2)}, u32[]{:S(2)}) collective-permute-start(f32[256,512]{1,0:T(8,128)S(1)} %convolution_add_fusion), channel_id=1, source_target_pairs={{0,16},{16,0},{1,17},{17,1},{2,18},{18,2},{3,19},{19,3},{4,20},{20... | collective-permute-start | bytes 1572872 | tf_op jit(solution)/shard_map/ppermute | solution.py:18
  (92 shorter events, 31.6 us)
Async XLA Ops:
  0.0 6.8 %collective-permute-start.1 = (bf16[256,512]{1,0:T(8,128)(2,1)}, bf16[256,512]{1,0:T(8,128)(2,1)S(1)}, u32[]{:S(2)}, u32[]{:S(2)}) collective-permute-start(bf16[256,512]{1,0:T(8,128)(2,1)} %param.1), channel_id=1, source_target_pairs={{0,16},{16,0},{1,17},{17,1},{2,18},{18,2},{3,19},{19,3},{4,20},{20... | collective-permute-start | bytes 786440 | tf_op jit(solution)/shard_map/ppermute | solution.py:18
  3.2 8.3 %collective-permute-start = (bf16[256,512]{1,0:T(8,128)(2,1)}, bf16[256,512]{1,0:T(8,128)(2,1)S(1)}, u32[]{:S(2)}, u32[]{:S(2)}) collective-permute-start(bf16[256,512]{1,0:T(8,128)(2,1)} %param.1), channel_id=1, source_target_pairs={{0,32},{32,0},{1,33},{33,1},{2,34},{34,2},{3,35},{35,3},{4,36},{36... | collective-permute-start | bytes 786440 | tf_op jit(solution)/shard_map/ppermute | solution.py:18
  3.2 9.9 %collective-permute-start.2 = (bf16[256,512]{1,0:T(8,128)(2,1)}, bf16[256,512]{1,0:T(8,128)(2,1)}, u32[]{:S(2)}, u32[]{:S(2)}) collective-permute-start(bf16[256,512]{1,0:T(8,128)(2,1)} %param.1), channel_id=1, source_target_pairs={{0,128},{64,192},{128,0},{192,64},{1,129},{65,193},{129,1},{193,65... | collective-permute-start | bytes 786440 | tf_op jit(solution)/shard_map/ppermute | solution.py:22
  11.5 13.0 %collective-permute-start.3 = (bf16[512,512]{1,0:T(8,128)(2,1)S(1)}, bf16[512,512]{1,0:T(8,128)(2,1)S(1)}, u32[]{:S(2)}, u32[]{:S(2)}) collective-permute-start(bf16[512,512]{1,0:T(8,128)(2,1)S(1)} %pad_maximum_fusion.3), channel_id=1, source_target_pairs={{0,64},{64,0},{128,192},{192,128},{1,65},{65,1},{129,193},{193,129... | collective-permute-start | bytes 1572872 | tf_op jit(solution)/shard_map/ppermute | solution.py:35
  11.6 14.2 %collective-permute-start.4 = (bf16[512,512]{1,0:T(8,128)(2,1)S(1)}, bf16[512,512]{1,0:T(8,128)(2,1)}, u32[]{:S(2)}, u32[]{:S(2)}) collective-permute-start(bf16[512,512]{1,0:T(8,128)(2,1)S(1)} %pad_maximum_fusion.3), channel_id=1, source_target_pairs={{0,192},{64,128},{128,64},{192,0},{1,193},{65,129},{129,65},{193,1... | collective-permute-start | bytes 1572872 | tf_op jit(solution)/shard_map/ppermute | solution.py:35
  14.2 7.1 %collective-permute-start.5 = (bf16[256,512]{1,0:T(8,128)(2,1)}, bf16[256,512]{1,0:T(8,128)(2,1)}, u32[]{:S(2)}, u32[]{:S(2)}) collective-permute-start(bf16[256,512]{1,0:T(8,128)(2,1)} %collective-permute-done.2), channel_id=1, source_target_pairs={{0,32},{32,0},{1,33},{33,1},{2,34},{34,2},{3,35},{35,3},{4,36},{36... | collective-permute-start | bytes 786440 | tf_op jit(solution)/shard_map/ppermute | solution.py:18
  17.2 17.0 %all-to-all-start = ((bf16[4,128,768]{2,1,0:T(8,128)(2,1)}), bf16[4,128,768]{2,1,0:T(8,128)(2,1)S(1)}, u32[]{:S(2)}, u32[]{:S(2)}) async-start(bf16[4,128,768]{2,1,0:T(8,128)(2,1)} %bitcast.25), calls=%async_computation | async-start | bytes 1572864 | tf_op jit(solution)/shard_map/all_to_all | solution.py:86
  28.9 9.6 %collective-permute-start.6 = (bf16[128,1280]{1,0:T(8,128)(2,1)}, bf16[128,1280]{1,0:T(8,128)(2,1)}, u32[]{:S(2)}, u32[]{:S(2)}) collective-permute-start(bf16[128,1280]{1,0:T(8,128)(2,1)} %convolution_convert_fusion.2), channel_id=1, source_target_pairs={{0,1},{1,0},{2,3},{3,2},{4,5},{5,4},{6,7},{7,6},{8,9},{9,8},{10,11... | collective-permute-start | bytes 983048 | tf_op jit(solution)/shard_map/ppermute | solution.py:35
  29.7 9.6 %collective-permute-start.7 = (bf16[128,1280]{1,0:T(8,128)(2,1)S(1)}, bf16[128,1280]{1,0:T(8,128)(2,1)}, u32[]{:S(2)}, u32[]{:S(2)}) collective-permute-start(bf16[128,1280]{1,0:T(8,128)(2,1)S(1)} %convolution_convert_fusion.1), channel_id=1, source_target_pairs={{0,3},{1,2},{2,1},{3,0},{4,7},{5,6},{6,5},{7,4},{8,11},{9,10},{10,... | collective-permute-start | bytes 983048 | tf_op jit(solution)/shard_map/ppermute | solution.py:35
  32.9 13.6 %collective-permute-start.8 = (bf16[128,1280]{1,0:T(8,128)(2,1)}, bf16[128,1280]{1,0:T(8,128)(2,1)}, u32[]{:S(2)}, u32[]{:S(2)}) collective-permute-start(bf16[128,1280]{1,0:T(8,128)(2,1)} %convolution_convert_fusion), channel_id=1, source_target_pairs={{0,2},{1,3},{2,0},{3,1},{4,6},{5,7},{6,4},{7,5},{8,10},{9,11},{10,... | collective-permute-start | bytes 983048 | tf_op jit(solution)/shard_map/ppermute | solution.py:35
  47.8 14.3 %collective-permute-start.10 = (bf16[32,2048]{1,0:T(8,128)(2,1)S(1)}, bf16[32,2048]{1,0:T(8,128)(2,1)S(1)}, u32[]{:S(2)}, u32[]{:S(2)}) collective-permute-start(bf16[32,2048]{1,0:T(8,128)(2,1)S(1)} %get-tuple-element.37), channel_id=1, source_target_pairs={{0,12},{4,8},{8,4},{12,0},{1,13},{5,9},{9,5},{13,1},{2,14},{6,10},... | collective-permute-start | bytes 393224 | tf_op jit(solution)/shard_map/ppermute | solution.py:35
  52.6 9.8 %collective-permute-start.11 = (bf16[32,2048]{1,0:T(8,128)(2,1)S(1)}, bf16[32,2048]{1,0:T(8,128)(2,1)S(1)}, u32[]{:S(2)}, u32[]{:S(2)}) collective-permute-start(bf16[32,2048]{1,0:T(8,128)(2,1)S(1)} %get-tuple-element.36), channel_id=1, source_target_pairs={{0,8},{4,12},{8,0},{12,4},{1,9},{5,13},{9,1},{13,5},{2,10},{6,14},... | collective-permute-start | bytes 393224 | tf_op jit(solution)/shard_map/ppermute | solution.py:35
  54.2 9.1 %collective-permute-start.9 = (bf16[32,2048]{1,0:T(8,128)(2,1)S(1)}, bf16[32,2048]{1,0:T(8,128)(2,1)}, u32[]{:S(2)}, u32[]{:S(2)}) collective-permute-start(bf16[32,2048]{1,0:T(8,128)(2,1)S(1)} %get-tuple-element.35), channel_id=1, source_target_pairs={{0,4},{4,0},{8,12},{12,8},{1,5},{5,1},{9,13},{13,9},{2,6},{6,2},{1... | collective-permute-start | bytes 393224 | tf_op jit(solution)/shard_map/ppermute | solution.py:35
  80.0 13.9 %collective-permute-start.12 = (bf16[128,2048]{1,0:T(8,128)(2,1)S(1)}, bf16[128,2048]{1,0:T(8,128)(2,1)S(1)}, u32[]{:S(2)}, u32[]{:S(2)}) collective-permute-start(bf16[128,2048]{1,0:T(8,128)(2,1)S(1)} %all_gather.3), channel_id=1, source_target_pairs={{0,3},{1,0},{2,1},{3,2},{4,7},{5,4},{6,5},{7,6},{8,11},{9,8},{10,9... | collective-permute-start | bytes 1572872 | tf_op jit(solution)/shard_map/ppermute | solution.py:22
  81.5 11.4 %collective-permute-start.13 = (bf16[128,2048]{1,0:T(8,128)(2,1)S(1)}, bf16[128,2048]{1,0:T(8,128)(2,1)S(1)}, u32[]{:S(2)}, u32[]{:S(2)}) collective-permute-start(bf16[128,2048]{1,0:T(8,128)(2,1)S(1)} %all_gather.3), channel_id=1, source_target_pairs={{0,1},{1,2},{2,3},{3,0},{4,5},{5,6},{6,7},{7,4},{8,9},{9,10},{10,1... | collective-permute-start | bytes 1572872 | tf_op jit(solution)/shard_map/ppermute | solution.py:22
  94.0 8.2 %collective-permute-start.15 = (bf16[64,2048]{1,0:T(8,128)(2,1)S(1)}, bf16[64,2048]{1,0:T(8,128)(2,1)S(1)}, u32[]{:S(2)}, u32[]{:S(2)}) collective-permute-start(bf16[64,2048]{1,0:T(8,128)(2,1)S(1)} %get-tuple-element.20), channel_id=1, source_target_pairs={{0,3},{1,0},{2,1},{3,2},{4,7},{5,4},{6,5},{7,6},{8,11},{9,8},{10,9... | collective-permute-start | bytes 786440 | tf_op jit(solution)/shard_map/ppermute | solution.py:22
  95.9 6.4 %collective-permute-start.16 = (bf16[64,2048]{1,0:T(8,128)(2,1)S(1)}, bf16[64,2048]{1,0:T(8,128)(2,1)S(1)}, u32[]{:S(2)}, u32[]{:S(2)}) collective-permute-start(bf16[64,2048]{1,0:T(8,128)(2,1)S(1)} %slice.85), channel_id=1, source_target_pairs={{0,1},{1,2},{2,3},{3,0},{4,5},{5,6},{6,7},{7,4},{8,9},{9,10},{10,1... | collective-permute-start | bytes 786440 | tf_op jit(solution)/shard_map/ppermute | solution.py:22
  96.9 11.8 %collective-permute-start.14 = (f32[192,512]{1,0:T(8,128)S(1)}, f32[192,512]{1,0:T(8,128)S(1)}, u32[]{:S(2)}, u32[]{:S(2)}) collective-permute-start(f32[192,512]{1,0:T(8,128)S(1)} %pad_maximum_fusion.8), channel_id=1, source_target_pairs={{0,16},{16,0},{1,17},{17,1},{2,18},{18,2},{3,19},{19,3},{4,20},{20... | collective-permute-start | bytes 1179656 | tf_op jit(solution)/shard_map/ppermute | solution.py:18
  102.9 6.7 %collective-permute-start.17 = (f32[64,512]{1,0:T(8,128)S(1)}, f32[64,512]{1,0:T(8,128)S(1)}, u32[]{:S(2)}, u32[]{:S(2)}) collective-permute-start(f32[64,512]{1,0:T(8,128)S(1)} %fusion.20), channel_id=1, source_target_pairs={{0,16},{16,0},{1,17},{17,1},{2,18},{18,2},{3,19},{19,3},{4,20},{20... | collective-permute-start | bytes 393224 | tf_op jit(solution)/shard_map/ppermute | solution.py:18
  110.2 7.6 %collective-permute-start.18 = (bf16[256,512]{1,0:T(8,128)(2,1)S(1)}, bf16[256,512]{1,0:T(8,128)(2,1)S(1)}, u32[]{:S(2)}, u32[]{:S(2)}) collective-permute-start(bf16[256,512]{1,0:T(8,128)(2,1)S(1)} %dynamic-slice_convert_fusion), channel_id=1, source_target_pairs={{0,32},{32,0},{1,33},{33,1},{2,34},{34,2},{3,35},{35,3},{4,36},{36... | collective-permute-start | bytes 786440 | tf_op jit(solution)/shard_map/ppermute | solution.py:18
  110.6 11.9 %collective-permute-start.19 = (bf16[256,512]{1,0:T(8,128)(2,1)S(1)}, bf16[256,512]{1,0:T(8,128)(2,1)S(1)}, u32[]{:S(2)}, u32[]{:S(2)}) collective-permute-start(bf16[256,512]{1,0:T(8,128)(2,1)S(1)} %dynamic-slice_convert_fusion), channel_id=1, source_target_pairs={{0,128},{64,192},{128,0},{192,64},{1,129},{65,193},{129,1},{193,65... | collective-permute-start | bytes 786440 | tf_op jit(solution)/shard_map/ppermute | solution.py:22
  117.9 13.4 %collective-permute-start.20 = (bf16[512,512]{1,0:T(8,128)(2,1)S(1)}, bf16[512,512]{1,0:T(8,128)(2,1)S(1)}, u32[]{:S(2)}, u32[]{:S(2)}) collective-permute-start(bf16[512,512]{1,0:T(8,128)(2,1)S(1)} %pad_maximum_fusion.7), channel_id=1, source_target_pairs={{0,64},{64,0},{128,192},{192,128},{1,65},{65,1},{129,193},{193,129... | collective-permute-start | bytes 1572872 | tf_op jit(solution)/shard_map/ppermute | solution.py:35
  119.0 14.3 %collective-permute-start.21 = (bf16[512,512]{1,0:T(8,128)(2,1)S(1)}, bf16[512,512]{1,0:T(8,128)(2,1)S(1)}, u32[]{:S(2)}, u32[]{:S(2)}) collective-permute-start(bf16[512,512]{1,0:T(8,128)(2,1)S(1)} %pad_maximum_fusion.7), channel_id=1, source_target_pairs={{0,192},{64,128},{128,64},{192,0},{1,193},{65,129},{129,65},{193,1... | collective-permute-start | bytes 1572872 | tf_op jit(solution)/shard_map/ppermute | solution.py:35
  122.6 6.0 %collective-permute-start.22 = (bf16[256,512]{1,0:T(8,128)(2,1)S(1)}, bf16[256,512]{1,0:T(8,128)(2,1)S(1)}, u32[]{:S(2)}, u32[]{:S(2)}) collective-permute-start(bf16[256,512]{1,0:T(8,128)(2,1)S(1)} %collective-permute-done.19), channel_id=1, source_target_pairs={{0,32},{32,0},{1,33},{33,1},{2,34},{34,2},{3,35},{35,3},{4,36},{36... | collective-permute-start | bytes 786440 | tf_op jit(solution)/shard_map/ppermute | solution.py:18
  (4 other events, 61.8 us)
where the time goes:
time: 140 us; the launch traced here: 139 us
  waiting for transfers between devices  53.2 us (38%)
  starting transfers between devices  53.1 us (38%)
  blocking collectives  15.8 us (11%)
  matrix products  10.1 us (7%)
  other arithmetic  5.01 us (4%)
  local copies, waits for them, and re-layouts  1.71 us (1%)
    ppermute x10, waiting for transfers between devices, trade(): return lax.ppermute(array, axis, [(i, i ^ k) for i in range(4)])  29.8 us
    ppermute x8, starting transfers between devices, swap(): return lax.ppermute(array, axis, [(0, 1), (1, 0)])  18.6 us
    ppermute x10, starting transfers between devices, trade(): return lax.ppermute(array, axis, [(i, i ^ k) for i in range(4)])  16.8 us
    all_gather x1, blocking collectives, per_device(): near = lax.all_gather(part, 'zh', axis=0, tiled=True)  15.8 us
    ppermute x8, waiting for transfers between devices, swap(): return lax.ppermute(array, axis, [(0, 1), (1, 0)])  14.8 us
    ppermute x6, starting transfers between devices, send(): lax.ppermute(array, axis, [(i, (i + k) % 4) for i in range(4)])  13.6 us
    dot_general x14, matrix products, matmul(): return lax.dot_general(a, b, (dims, ((), ())), preferred_element_type=F32)  10.1 us
    ppermute x6, waiting for transfers between devices, send(): lax.ppermute(array, axis, [(i, (i + k) % 4) for i in range(4)])  8.59 us
  transfers between devices with their start and end apart: 25, of which 18 were waited for; matrix products, arithmetic and copies ran while one was open for 8% of the time, Pallas kernels for 0%

commit v1 on v0

--- a/solution.py
+++ b/solution.py
@@ -91,7 +91,9 @@
     part = jnp.concatenate([first, second], axis=1)
     panel = jnp.concatenate([early, panel], axis=0)
     part = add(scatter_pairs(chunks(part), "zh"))
-    near = lax.all_gather(part, "zh", axis=0, tiled=True)
+    near = jnp.concatenate(
+        lax.all_to_all(jnp.stack([part] * lax.axis_size("zh")), "zh", 0, 0), axis=0
+    )
     after, before = (fetch(near, "y", 1), fetch(near, "y", 3))
     sent = lax.optimization_barrier((after[:64], before[64:]))
     far = lax.optimization_barrier((fetch(sent[0], "y", 1), fetch(sent[1], "y", 3)))

time: 140 us -> 144 us (1.029)
  waiting for transfers between devices: 53.2 us -> 77.3 us
  blocking collectives: 15.8 us -> 0 us
  starting transfers between devices: 53.1 us -> 49.2 us
    all_gather x1 -> x0, blocking collectives: 15.8 us -> none  [per_device(): near = lax.all_gather(part, 'zh', axis=0, tiled=True)]
    all_to_all x0 -> x1, waiting for transfers between devices: none -> 11.5 us  [per_device(): lax.all_to_all(jnp.stack([part] * lax.axis_size('zh')), 'zh', 0, 0)]
    ppermute x6, waiting for transfers between devices: 8.59 us -> 16.5 us  [send(): lax.ppermute(array, axis, [(i, (i + k) % 4) for i in range(4)])]
    all_to_all x0 -> x1, starting transfers between devices: none -> 6.36 us  [per_device(): lax.all_to_all(jnp.stack([part] * lax.axis_size('zh')), 'zh', 0, 0)]
    ppermute x8, starting transfers between devices: 18.6 us -> 13 us  [swap(): return lax.ppermute(array, axis, [(0, 1), (1, 0)])]
    ppermute x10, starting transfers between devices: 16.8 us -> 12.2 us  [trade(): return lax.ppermute(array, axis, [(i, i ^ k) for i in range(4)])]
    ppermute x8, waiting for transfers between devices: 14.8 us -> 18 us  [swap(): return lax.ppermute(array, axis, [(0, 1), (1, 0)])]
    ppermute x10, waiting for transfers between devices: 29.8 us -> 31.3 us  [trade(): return lax.ppermute(array, axis, [(i, i ^ k) for i in range(4)])]
  transfers between devices with their start and end apart: 25 -> 26, of which waited for: 18 -> 21; matrix products, arithmetic and copies ran while one was open for 8% -> 8% of each run, Pallas kernels for 0% -> 0%
where the time goes in v1:
time: 144 us
  waiting for transfers between devices  77.3 us (54%)
  starting transfers between devices  49.2 us (34%)
  matrix products  10.1 us (7%)
  other arithmetic  4.11 us (3%)
  local copies, waits for them, and re-layouts  2.59 us (2%)
    ppermute x10, waiting for transfers between devices, trade(): return lax.ppermute(array, axis, [(i, i ^ k) for i in range(4)])  31.3 us
    ppermute x8, waiting for transfers between devices, swap(): return lax.ppermute(array, axis, [(0, 1), (1, 0)])  18 us
    ppermute x6, waiting for transfers between devices, send(): lax.ppermute(array, axis, [(i, (i + k) % 4) for i in range(4)])  16.5 us
    ppermute x6, starting transfers between devices, send(): lax.ppermute(array, axis, [(i, (i + k) % 4) for i in range(4)])  13.5 us
    ppermute x8, starting transfers between devices, swap(): return lax.ppermute(array, axis, [(0, 1), (1, 0)])  13 us
    ppermute x10, starting transfers between devices, trade(): return lax.ppermute(array, axis, [(i, i ^ k) for i in range(4)])  12.2 us
    all_to_all x1, waiting for transfers between devices, per_device(): lax.all_to_all(jnp.stack([part] * lax.axis_size('zh')), 'zh', 0, 0)  11.5 us
    dot_general x14, matrix products, matmul(): return lax.dot_general(a, b, (dims, ((), ())), preferred_element_type=F32)  10.1 us
  transfers between devices with their start and end apart: 26, of which 21 were waited for; matrix products, arithmetic and copies ran while one was open for 8% of the time, Pallas kernels for 0%

profile of v1, /device:TPU:1, one launch (start us, length us, event | category | flops | bytes accessed | tf_op | source)
XLA Modules:
  0.0 143.8 jit_solution(15963387889569627992)
XLA Ops:
  0.0 3.2 %collective-permute-start.1 = (bf16[256,512]{1,0:T(8,128)(2,1)}, bf16[256,512]{1,0:T(8,128)(2,1)S(1)}, u32[]{:S(2)}, u32[]{:S(2)}) collective-permute-start(bf16[256,512]{1,0:T(8,128)(2,1)} %param.1), channel_id=1, source_target_pairs={{0,16},{16,0},{1,17},{17,1},{2,18},{18,2},{3,19},{19,3},{4,20},{20... | collective-permute-start | bytes 786440 | tf_op jit(solution)/shard_map/ppermute | solution.py:18
  3.2 2.6 %collective-permute-start.2 = (bf16[256,512]{1,0:T(8,128)(2,1)}, bf16[256,512]{1,0:T(8,128)(2,1)}, u32[]{:S(2)}, u32[]{:S(2)}) collective-permute-start(bf16[256,512]{1,0:T(8,128)(2,1)} %param.1), channel_id=1, source_target_pairs={{0,128},{64,192},{128,0},{192,64},{1,129},{65,193},{129,1},{193,65... | collective-permute-start | bytes 786440 | tf_op jit(solution)/shard_map/ppermute | solution.py:22
  7.3 4.2 %collective-permute-done = bf16[256,512]{1,0:T(8,128)(2,1)S(1)} collective-permute-done((bf16[256,512]{1,0:T(8,128)(2,1)}, bf16[256,512]{1,0:T(8,128)(2,1)S(1)}, u32[]{:S(2)}, u32[]{:S(2)}) %collective-permute-start) | collective-permute-done | bytes 262176 | tf_op jit(solution)/shard_map/ppermute | solution.py:18
  17.2 4.2 %all-to-all-start = ((bf16[4,128,768]{2,1,0:T(8,128)(2,1)}), bf16[4,128,768]{2,1,0:T(8,128)(2,1)S(1)}, u32[]{:S(2)}, u32[]{:S(2)}) async-start(bf16[4,128,768]{2,1,0:T(8,128)(2,1)} %bitcast.35), calls=%async_computation | async-start | bytes 1572864 | tf_op jit(solution)/shard_map/all_to_all | solution.py:86
  21.3 3.2 %collective-permute-done.3 = bf16[512,512]{1,0:T(8,128)(2,1)S(1)} collective-permute-done((bf16[512,512]{1,0:T(8,128)(2,1)S(1)}, bf16[512,512]{1,0:T(8,128)(2,1)S(1)}, u32[]{:S(2)}, u32[]{:S(2)}) %collective-permute-start.3) | collective-permute-done | bytes 524320 | tf_op jit(solution)/shard_map/ppermute | solution.py:35
  29.7 1.9 %collective-permute-start.7 = (bf16[128,1280]{1,0:T(8,128)(2,1)S(1)}, bf16[128,1280]{1,0:T(8,128)(2,1)}, u32[]{:S(2)}, u32[]{:S(2)}) collective-permute-start(bf16[128,1280]{1,0:T(8,128)(2,1)S(1)} %convolution_convert_fusion.1), channel_id=1, source_target_pairs={{0,3},{1,2},{2,1},{3,0},{4,7},{5,6},{6,5},{7,4},{8,11},{9,10},{10,... | collective-permute-start | bytes 983048 | tf_op jit(solution)/shard_map/ppermute | solution.py:35
  34.3 4.3 %collective-permute-done.6 = bf16[128,1280]{1,0:T(8,128)(2,1)} collective-permute-done((bf16[128,1280]{1,0:T(8,128)(2,1)}, bf16[128,1280]{1,0:T(8,128)(2,1)}, u32[]{:S(2)}, u32[]{:S(2)}) %collective-permute-start.6) | collective-permute-done | bytes 327712 | tf_op jit(solution)/shard_map/ppermute | solution.py:35
  39.3 7.1 %collective-permute-done.8 = bf16[128,1280]{1,0:T(8,128)(2,1)} collective-permute-done((bf16[128,1280]{1,0:T(8,128)(2,1)}, bf16[128,1280]{1,0:T(8,128)(2,1)}, u32[]{:S(2)}, u32[]{:S(2)}) %collective-permute-start.8) | collective-permute-done | bytes 327712 | tf_op jit(solution)/shard_map/ppermute | solution.py:35
  47.8 4.8 %collective-permute-start.10 = (bf16[32,2048]{1,0:T(8,128)(2,1)S(1)}, bf16[32,2048]{1,0:T(8,128)(2,1)S(1)}, u32[]{:S(2)}, u32[]{:S(2)}) collective-permute-start(bf16[32,2048]{1,0:T(8,128)(2,1)S(1)} %get-tuple-element.37), channel_id=1, source_target_pairs={{0,12},{4,8},{8,4},{12,0},{1,13},{5,9},{9,5},{13,1},{2,14},{6,10},... | collective-permute-start | bytes 393224 | tf_op jit(solution)/shard_map/ppermute | solution.py:35
  54.8 7.3 %collective-permute-done.10 = bf16[32,2048]{1,0:T(8,128)(2,1)S(1)} collective-permute-done((bf16[32,2048]{1,0:T(8,128)(2,1)S(1)}, bf16[32,2048]{1,0:T(8,128)(2,1)S(1)}, u32[]{:S(2)}, u32[]{:S(2)}) %collective-permute-start.10) | collective-permute-done | bytes 131104 | tf_op jit(solution)/shard_map/ppermute | solution.py:35
  64.1 6.4 %all-to-all-start.1 = ((bf16[4,32,2048]{2,1,0:T(8,128)(2,1)}), bf16[4,32,2048]{2,1,0:T(8,128)(2,1)S(1)}, u32[]{:S(2)}, u32[]{:S(2)}) async-start(bf16[4,32,2048]{2,1,0:T(8,128)(2,1)} %stack.27), calls=%async_computation.1 | async-start | bytes 1048576 | tf_op jit(solution)/shard_map/all_to_all | solution.py:95
  70.5 11.5 %all-to-all-done.1 = bf16[4,32,2048]{2,1,0:T(8,128)(2,1)S(1)} async-done(((bf16[4,32,2048]{2,1,0:T(8,128)(2,1)}), bf16[4,32,2048]{2,1,0:T(8,128)(2,1)S(1)}, u32[]{:S(2)}, u32[]{:S(2)}) %all-to-all-start.1) | async-done | bytes 524320 | tf_op jit(solution)/shard_map/all_to_all | solution.py:95
  81.9 1.7 %collective-permute-start.12 = (bf16[128,2048]{1,0:T(8,128)(2,1)S(1)}, bf16[128,2048]{1,0:T(8,128)(2,1)S(1)}, u32[]{:S(2)}, u32[]{:S(2)}) collective-permute-start(bf16[128,2048]{1,0:T(8,128)(2,1)S(1)} %bitcast.30), channel_id=1, source_target_pairs={{0,3},{1,0},{2,1},{3,2},{4,7},{5,4},{6,5},{7,6},{8,11},{9,8},{10,9... | collective-permute-start | bytes 1572872 | tf_op jit(solution)/shard_map/ppermute | solution.py:22
  83.7 7.1 %collective-permute-start.13 = (bf16[128,2048]{1,0:T(8,128)(2,1)S(1)}, bf16[128,2048]{1,0:T(8,128)(2,1)S(1)}, u32[]{:S(2)}, u32[]{:S(2)}) collective-permute-start(bf16[128,2048]{1,0:T(8,128)(2,1)S(1)} %bitcast.31), channel_id=1, source_target_pairs={{0,1},{1,2},{2,3},{3,0},{4,5},{5,6},{6,7},{7,4},{8,9},{9,10},{10,1... | collective-permute-start | bytes 1572872 | tf_op jit(solution)/shard_map/ppermute | solution.py:22
  91.4 9.9 %collective-permute-done.13 = bf16[128,2048]{1,0:T(8,128)(2,1)S(1)} collective-permute-done((bf16[128,2048]{1,0:T(8,128)(2,1)S(1)}, bf16[128,2048]{1,0:T(8,128)(2,1)S(1)}, u32[]{:S(2)}, u32[]{:S(2)}) %collective-permute-start.13) | collective-permute-done | bytes 524320 | tf_op jit(solution)/shard_map/ppermute | solution.py:22
  102.4 1.9 %collective-permute-start.15 = (bf16[64,2048]{1,0:T(8,128)(2,1)S(1)}, bf16[64,2048]{1,0:T(8,128)(2,1)S(1)}, u32[]{:S(2)}, u32[]{:S(2)}) collective-permute-start(bf16[64,2048]{1,0:T(8,128)(2,1)S(1)} %get-tuple-element.20), channel_id=1, source_target_pairs={{0,3},{1,0},{2,1},{3,2},{4,7},{5,4},{6,5},{7,6},{8,11},{9,8},{10,9... | collective-permute-start | bytes 786440 | tf_op jit(solution)/shard_map/ppermute | solution.py:22
  105.3 2.0 %collective-permute-start.14 = (f32[192,512]{1,0:T(8,128)S(1)}, f32[192,512]{1,0:T(8,128)S(1)}, u32[]{:S(2)}, u32[]{:S(2)}) collective-permute-start(f32[192,512]{1,0:T(8,128)S(1)} %pad_maximum_fusion.8), channel_id=1, source_target_pairs={{0,16},{16,0},{1,17},{17,1},{2,18},{18,2},{3,19},{19,3},{4,20},{20... | collective-permute-start | bytes 1179656 | tf_op jit(solution)/shard_map/ppermute | solution.py:18
  107.3 1.7 %collective-permute-done.15 = bf16[64,2048]{1,0:T(8,128)(2,1)S(1)} collective-permute-done((bf16[64,2048]{1,0:T(8,128)(2,1)S(1)}, bf16[64,2048]{1,0:T(8,128)(2,1)S(1)}, u32[]{:S(2)}, u32[]{:S(2)}) %collective-permute-start.15) | collective-permute-done | bytes 262176 | tf_op jit(solution)/shard_map/ppermute | solution.py:22
  109.0 2.4 %collective-permute-done.16 = bf16[64,2048]{1,0:T(8,128)(2,1)S(1)} collective-permute-done((bf16[64,2048]{1,0:T(8,128)(2,1)S(1)}, bf16[64,2048]{1,0:T(8,128)(2,1)S(1)}, u32[]{:S(2)}, u32[]{:S(2)}) %collective-permute-start.16) | collective-permute-done | bytes 262176 | tf_op jit(solution)/shard_map/ppermute | solution.py:22
  112.0 2.9 %collective-permute-start.17 = (f32[64,512]{1,0:T(8,128)S(1)}, f32[64,512]{1,0:T(8,128)S(1)}, u32[]{:S(2)}, u32[]{:S(2)}) collective-permute-start(f32[64,512]{1,0:T(8,128)S(1)} %fusion.20), channel_id=1, source_target_pairs={{0,16},{16,0},{1,17},{17,1},{2,18},{18,2},{3,19},{19,3},{4,20},{20... | collective-permute-start | bytes 393224 | tf_op jit(solution)/shard_map/ppermute | solution.py:18
  116.7 7.4 %collective-permute-done.18 = bf16[256,512]{1,0:T(8,128)(2,1)S(1)} collective-permute-done((bf16[256,512]{1,0:T(8,128)(2,1)S(1)}, bf16[256,512]{1,0:T(8,128)(2,1)S(1)}, u32[]{:S(2)}, u32[]{:S(2)}) %collective-permute-start.18) | collective-permute-done | bytes 262176 | tf_op jit(solution)/shard_map/ppermute | solution.py:18
  126.9 4.6 %collective-permute-done.22 = bf16[256,512]{1,0:T(8,128)(2,1)S(1)} collective-permute-done((bf16[256,512]{1,0:T(8,128)(2,1)S(1)}, bf16[256,512]{1,0:T(8,128)(2,1)S(1)}, u32[]{:S(2)}, u32[]{:S(2)}) %collective-permute-start.22) | collective-permute-done | bytes 262176 | tf_op jit(solution)/shard_map/ppermute | solution.py:18
  131.5 4.9 %collective-permute-done.20 = bf16[512,512]{1,0:T(8,128)(2,1)S(1)} collective-permute-done((bf16[512,512]{1,0:T(8,128)(2,1)S(1)}, bf16[512,512]{1,0:T(8,128)(2,1)S(1)}, u32[]{:S(2)}, u32[]{:S(2)}) %collective-permute-start.20) | collective-permute-done | bytes 524320 | tf_op jit(solution)/shard_map/ppermute | solution.py:35
  138.8 2.2 %collective-permute-start.23 = (f32[256,512]{1,0:T(8,128)S(1)}, f32[256,512]{1,0:T(8,128)S(1)}, u32[]{:S(2)}, u32[]{:S(2)}) collective-permute-start(f32[256,512]{1,0:T(8,128)S(1)} %convolution_add_fusion), channel_id=1, source_target_pairs={{0,16},{16,0},{1,17},{17,1},{2,18},{18,2},{3,19},{19,3},{4,20},{20... | collective-permute-start | bytes 1572872 | tf_op jit(solution)/shard_map/ppermute | solution.py:18
  (96 shorter events, 33.8 us)
Async XLA Ops:
  0.0 6.8 %collective-permute-start.1 = (bf16[256,512]{1,0:T(8,128)(2,1)}, bf16[256,512]{1,0:T(8,128)(2,1)S(1)}, u32[]{:S(2)}, u32[]{:S(2)}) collective-permute-start(bf16[256,512]{1,0:T(8,128)(2,1)} %param.1), channel_id=1, source_target_pairs={{0,16},{16,0},{1,17},{17,1},{2,18},{18,2},{3,19},{19,3},{4,20},{20... | collective-permute-start | bytes 786440 | tf_op jit(solution)/shard_map/ppermute | solution.py:18
  3.2 8.3 %collective-permute-start = (bf16[256,512]{1,0:T(8,128)(2,1)}, bf16[256,512]{1,0:T(8,128)(2,1)S(1)}, u32[]{:S(2)}, u32[]{:S(2)}) collective-permute-start(bf16[256,512]{1,0:T(8,128)(2,1)} %param.1), channel_id=1, source_target_pairs={{0,32},{32,0},{1,33},{33,1},{2,34},{34,2},{3,35},{35,3},{4,36},{36... | collective-permute-start | bytes 786440 | tf_op jit(solution)/shard_map/ppermute | solution.py:18
  3.2 9.9 %collective-permute-start.2 = (bf16[256,512]{1,0:T(8,128)(2,1)}, bf16[256,512]{1,0:T(8,128)(2,1)}, u32[]{:S(2)}, u32[]{:S(2)}) collective-permute-start(bf16[256,512]{1,0:T(8,128)(2,1)} %param.1), channel_id=1, source_target_pairs={{0,128},{64,192},{128,0},{192,64},{1,129},{65,193},{129,1},{193,65... | collective-permute-start | bytes 786440 | tf_op jit(solution)/shard_map/ppermute | solution.py:22
  11.5 13.0 %collective-permute-start.3 = (bf16[512,512]{1,0:T(8,128)(2,1)S(1)}, bf16[512,512]{1,0:T(8,128)(2,1)S(1)}, u32[]{:S(2)}, u32[]{:S(2)}) collective-permute-start(bf16[512,512]{1,0:T(8,128)(2,1)S(1)} %pad_maximum_fusion.3), channel_id=1, source_target_pairs={{0,64},{64,0},{128,192},{192,128},{1,65},{65,1},{129,193},{193,129... | collective-permute-start | bytes 1572872 | tf_op jit(solution)/shard_map/ppermute | solution.py:35
  11.6 14.2 %collective-permute-start.4 = (bf16[512,512]{1,0:T(8,128)(2,1)S(1)}, bf16[512,512]{1,0:T(8,128)(2,1)}, u32[]{:S(2)}, u32[]{:S(2)}) collective-permute-start(bf16[512,512]{1,0:T(8,128)(2,1)S(1)} %pad_maximum_fusion.3), channel_id=1, source_target_pairs={{0,192},{64,128},{128,64},{192,0},{1,193},{65,129},{129,65},{193,1... | collective-permute-start | bytes 1572872 | tf_op jit(solution)/shard_map/ppermute | solution.py:35
  14.2 7.1 %collective-permute-start.5 = (bf16[256,512]{1,0:T(8,128)(2,1)}, bf16[256,512]{1,0:T(8,128)(2,1)}, u32[]{:S(2)}, u32[]{:S(2)}) collective-permute-start(bf16[256,512]{1,0:T(8,128)(2,1)} %collective-permute-done.2), channel_id=1, source_target_pairs={{0,32},{32,0},{1,33},{33,1},{2,34},{34,2},{3,35},{35,3},{4,36},{36... | collective-permute-start | bytes 786440 | tf_op jit(solution)/shard_map/ppermute | solution.py:18
  17.2 17.0 %all-to-all-start = ((bf16[4,128,768]{2,1,0:T(8,128)(2,1)}), bf16[4,128,768]{2,1,0:T(8,128)(2,1)S(1)}, u32[]{:S(2)}, u32[]{:S(2)}) async-start(bf16[4,128,768]{2,1,0:T(8,128)(2,1)} %bitcast.35), calls=%async_computation | async-start | bytes 1572864 | tf_op jit(solution)/shard_map/all_to_all | solution.py:86
  28.9 9.6 %collective-permute-start.6 = (bf16[128,1280]{1,0:T(8,128)(2,1)}, bf16[128,1280]{1,0:T(8,128)(2,1)}, u32[]{:S(2)}, u32[]{:S(2)}) collective-permute-start(bf16[128,1280]{1,0:T(8,128)(2,1)} %convolution_convert_fusion.2), channel_id=1, source_target_pairs={{0,1},{1,0},{2,3},{3,2},{4,5},{5,4},{6,7},{7,6},{8,9},{9,8},{10,11... | collective-permute-start | bytes 983048 | tf_op jit(solution)/shard_map/ppermute | solution.py:35
  29.7 9.6 %collective-permute-start.7 = (bf16[128,1280]{1,0:T(8,128)(2,1)S(1)}, bf16[128,1280]{1,0:T(8,128)(2,1)}, u32[]{:S(2)}, u32[]{:S(2)}) collective-permute-start(bf16[128,1280]{1,0:T(8,128)(2,1)S(1)} %convolution_convert_fusion.1), channel_id=1, source_target_pairs={{0,3},{1,2},{2,1},{3,0},{4,7},{5,6},{6,5},{7,4},{8,11},{9,10},{10,... | collective-permute-start | bytes 983048 | tf_op jit(solution)/shard_map/ppermute | solution.py:35
  32.9 13.6 %collective-permute-start.8 = (bf16[128,1280]{1,0:T(8,128)(2,1)}, bf16[128,1280]{1,0:T(8,128)(2,1)}, u32[]{:S(2)}, u32[]{:S(2)}) collective-permute-start(bf16[128,1280]{1,0:T(8,128)(2,1)} %convolution_convert_fusion), channel_id=1, source_target_pairs={{0,2},{1,3},{2,0},{3,1},{4,6},{5,7},{6,4},{7,5},{8,10},{9,11},{10,... | collective-permute-start | bytes 983048 | tf_op jit(solution)/shard_map/ppermute | solution.py:35
  47.8 14.3 %collective-permute-start.10 = (bf16[32,2048]{1,0:T(8,128)(2,1)S(1)}, bf16[32,2048]{1,0:T(8,128)(2,1)S(1)}, u32[]{:S(2)}, u32[]{:S(2)}) collective-permute-start(bf16[32,2048]{1,0:T(8,128)(2,1)S(1)} %get-tuple-element.37), channel_id=1, source_target_pairs={{0,12},{4,8},{8,4},{12,0},{1,13},{5,9},{9,5},{13,1},{2,14},{6,10},... | collective-permute-start | bytes 393224 | tf_op jit(solution)/shard_map/ppermute | solution.py:35
  52.6 9.8 %collective-permute-start.11 = (bf16[32,2048]{1,0:T(8,128)(2,1)S(1)}, bf16[32,2048]{1,0:T(8,128)(2,1)S(1)}, u32[]{:S(2)}, u32[]{:S(2)}) collective-permute-start(bf16[32,2048]{1,0:T(8,128)(2,1)S(1)} %get-tuple-element.36), channel_id=1, source_target_pairs={{0,8},{4,12},{8,0},{12,4},{1,9},{5,13},{9,1},{13,5},{2,10},{6,14},... | collective-permute-start | bytes 393224 | tf_op jit(solution)/shard_map/ppermute | solution.py:35
  54.2 9.0 %collective-permute-start.9 = (bf16[32,2048]{1,0:T(8,128)(2,1)S(1)}, bf16[32,2048]{1,0:T(8,128)(2,1)S(1)}, u32[]{:S(2)}, u32[]{:S(2)}) collective-permute-start(bf16[32,2048]{1,0:T(8,128)(2,1)S(1)} %get-tuple-element.35), channel_id=1, source_target_pairs={{0,4},{4,0},{8,12},{12,8},{1,5},{5,1},{9,13},{13,9},{2,6},{6,2},{1... | collective-permute-start | bytes 393224 | tf_op jit(solution)/shard_map/ppermute | solution.py:35
  64.1 17.8 %all-to-all-start.1 = ((bf16[4,32,2048]{2,1,0:T(8,128)(2,1)}), bf16[4,32,2048]{2,1,0:T(8,128)(2,1)S(1)}, u32[]{:S(2)}, u32[]{:S(2)}) async-start(bf16[4,32,2048]{2,1,0:T(8,128)(2,1)} %stack.27), calls=%async_computation.1 | async-start | bytes 1048576 | tf_op jit(solution)/shard_map/all_to_all | solution.py:95
  81.9 20.4 %collective-permute-start.12 = (bf16[128,2048]{1,0:T(8,128)(2,1)S(1)}, bf16[128,2048]{1,0:T(8,128)(2,1)S(1)}, u32[]{:S(2)}, u32[]{:S(2)}) collective-permute-start(bf16[128,2048]{1,0:T(8,128)(2,1)S(1)} %bitcast.30), channel_id=1, source_target_pairs={{0,3},{1,0},{2,1},{3,2},{4,7},{5,4},{6,5},{7,6},{8,11},{9,8},{10,9... | collective-permute-start | bytes 1572872 | tf_op jit(solution)/shard_map/ppermute | solution.py:22
  83.7 17.7 %collective-permute-start.13 = (bf16[128,2048]{1,0:T(8,128)(2,1)S(1)}, bf16[128,2048]{1,0:T(8,128)(2,1)S(1)}, u32[]{:S(2)}, u32[]{:S(2)}) collective-permute-start(bf16[128,2048]{1,0:T(8,128)(2,1)S(1)} %bitcast.31), channel_id=1, source_target_pairs={{0,1},{1,2},{2,3},{3,0},{4,5},{5,6},{6,7},{7,4},{8,9},{9,10},{10,1... | collective-permute-start | bytes 1572872 | tf_op jit(solution)/shard_map/ppermute | solution.py:22
  102.4 6.6 %collective-permute-start.15 = (bf16[64,2048]{1,0:T(8,128)(2,1)S(1)}, bf16[64,2048]{1,0:T(8,128)(2,1)S(1)}, u32[]{:S(2)}, u32[]{:S(2)}) collective-permute-start(bf16[64,2048]{1,0:T(8,128)(2,1)S(1)} %get-tuple-element.20), channel_id=1, source_target_pairs={{0,3},{1,0},{2,1},{3,2},{4,7},{5,4},{6,5},{7,6},{8,11},{9,8},{10,9... | collective-permute-start | bytes 786440 | tf_op jit(solution)/shard_map/ppermute | solution.py:22
  104.3 7.1 %collective-permute-start.16 = (bf16[64,2048]{1,0:T(8,128)(2,1)S(1)}, bf16[64,2048]{1,0:T(8,128)(2,1)S(1)}, u32[]{:S(2)}, u32[]{:S(2)}) collective-permute-start(bf16[64,2048]{1,0:T(8,128)(2,1)S(1)} %slice.93), channel_id=1, source_target_pairs={{0,1},{1,2},{2,3},{3,0},{4,5},{5,6},{6,7},{7,4},{8,9},{9,10},{10,1... | collective-permute-start | bytes 786440 | tf_op jit(solution)/shard_map/ppermute | solution.py:22
  105.3 9.7 %collective-permute-start.14 = (f32[192,512]{1,0:T(8,128)S(1)}, f32[192,512]{1,0:T(8,128)S(1)}, u32[]{:S(2)}, u32[]{:S(2)}) collective-permute-start(f32[192,512]{1,0:T(8,128)S(1)} %pad_maximum_fusion.8), channel_id=1, source_target_pairs={{0,16},{16,0},{1,17},{17,1},{2,18},{18,2},{3,19},{19,3},{4,20},{20... | collective-permute-start | bytes 1179656 | tf_op jit(solution)/shard_map/ppermute | solution.py:18
  116.5 7.6 %collective-permute-start.18 = (bf16[256,512]{1,0:T(8,128)(2,1)S(1)}, bf16[256,512]{1,0:T(8,128)(2,1)S(1)}, u32[]{:S(2)}, u32[]{:S(2)}) collective-permute-start(bf16[256,512]{1,0:T(8,128)(2,1)S(1)} %dynamic-slice_convert_fusion), channel_id=1, source_target_pairs={{0,32},{32,0},{1,33},{33,1},{2,34},{34,2},{3,35},{35,3},{4,36},{36... | collective-permute-start | bytes 786440 | tf_op jit(solution)/shard_map/ppermute | solution.py:18
  116.6 9.1 %collective-permute-start.19 = (bf16[256,512]{1,0:T(8,128)(2,1)S(1)}, bf16[256,512]{1,0:T(8,128)(2,1)S(1)}, u32[]{:S(2)}, u32[]{:S(2)}) collective-permute-start(bf16[256,512]{1,0:T(8,128)(2,1)S(1)} %dynamic-slice_convert_fusion), channel_id=1, source_target_pairs={{0,128},{64,192},{128,0},{192,64},{1,129},{65,193},{129,1},{193,65... | collective-permute-start | bytes 786440 | tf_op jit(solution)/shard_map/ppermute | solution.py:22
  124.1 12.3 %collective-permute-start.20 = (bf16[512,512]{1,0:T(8,128)(2,1)S(1)}, bf16[512,512]{1,0:T(8,128)(2,1)S(1)}, u32[]{:S(2)}, u32[]{:S(2)}) collective-permute-start(bf16[512,512]{1,0:T(8,128)(2,1)S(1)} %pad_maximum_fusion.7), channel_id=1, source_target_pairs={{0,64},{64,0},{128,192},{192,128},{1,65},{65,1},{129,193},{193,129... | collective-permute-start | bytes 1572872 | tf_op jit(solution)/shard_map/ppermute | solution.py:35
  124.2 13.5 %collective-permute-start.21 = (bf16[512,512]{1,0:T(8,128)(2,1)S(1)}, bf16[512,512]{1,0:T(8,128)(2,1)S(1)}, u32[]{:S(2)}, u32[]{:S(2)}) collective-permute-start(bf16[512,512]{1,0:T(8,128)(2,1)S(1)} %pad_maximum_fusion.7), channel_id=1, source_target_pairs={{0,192},{64,128},{128,64},{192,0},{1,193},{65,129},{129,65},{193,1... | collective-permute-start | bytes 1572872 | tf_op jit(solution)/shard_map/ppermute | solution.py:35
  125.7 5.8 %collective-permute-start.22 = (bf16[256,512]{1,0:T(8,128)(2,1)S(1)}, bf16[256,512]{1,0:T(8,128)(2,1)S(1)}, u32[]{:S(2)}, u32[]{:S(2)}) collective-permute-start(bf16[256,512]{1,0:T(8,128)(2,1)S(1)} %collective-permute-done.19), channel_id=1, source_target_pairs={{0,32},{32,0},{1,33},{33,1},{2,34},{34,2},{3,35},{35,3},{4,36},{36... | collective-permute-start | bytes 786440 | tf_op jit(solution)/shard_map/ppermute | solution.py:18
  (5 other events, 42.7 us)
